TPU v7x, 256 devices: a whole 4x4x8 slice. The times are simulated.
256 devices in a mesh: seq: 32 (over y, x, core), tp: 8 (over z).
Axes of the slice: x: 4, y: 4, z: 8, core: 2. Of those that a mesh axis runs over, the one named last changes fastest.
Arguments:
- tokens: bfloat16 [8192, 4096], P('seq', 'tp'), may hold values from -11 to 11
- grad_out: bfloat16 [8192, 4096], P('seq', 'tp'), may hold values from -1.5 to 1.5
- in_weight: bfloat16 [4096, 4096], P('seq', 'tp'), may hold values from -0.09880682 to 0.09880682
- in_scale: float32 [4096], P('tp'), may hold values from 0.0008238636 to 0.010511364
- out_weight: bfloat16 [4096, 4096], P('seq', 'tp'), may hold values from -0.053943182 to 0.053943182
- out_scale: float32 [4096], replicated, may hold values from 0.00139204545 to 0.0057386364
- state_in: bfloat16 [8192, 128], P('seq'), may hold values from -0.0625 to 0.0625
- state_out: bfloat16 [8192, 128], P('seq'), may hold values from -6 to 6
- log_decay: float32 [8192, 64], P('seq', 'tp'), may hold values from -1.6 to 0
Outputs:
- grad_tokens: bfloat16 [8192, 4096], P('seq', 'tp')
- grad_in_weight: float32 [4096, 4096], P('seq', 'tp')
- grad_in_scale: float32 [4096], P('tp')
- grad_out_weight: float32 [4096, 4096], P('seq', 'tp')
- grad_out_scale: float32 [4096], P('seq')
All inputs are finite; a program needn't handle non-finite values.
Results may differ from a plain program's by a relative error of at most 0.027.
Values may be sent and summed in bfloat16 or wider, within the bound.
No kernel may reach another device: no remote copies, remote signals or barrier semaphores. Data moves between devices by JAX's collectives and lax.ppermute only.
A program may use at most 128 MiB of HBM per device.

v0:
```python
import jax
import jax.numpy as jnp
from jax import lax
from jax.sharding import PartitionSpec as P

D = 4096
HEADS = 64
HEAD_DIM = 64
STRETCH = 256
QMAX = 7
precise = lax.Precision.HIGHEST


def prefix(array, axis, join, neutral, backward):
    count = lax.axis_size(axis)
    place = lax.axis_index(axis)
    ahead = count - 1 - place if backward else place
    gathered = jax.tree.map(
        lambda a, kind: lax.all_gather(a.astype(kind), axis), array, (jnp.bfloat16, jnp.bfloat16)
    )
    state = jax.tree.map(lambda a, e: jnp.zeros_like(a) + jnp.asarray(e, a.dtype), array, neutral)

    def one(turn, state):
        source = count - 1 - turn if backward else turn
        return join(
            state,
            jax.tree.map(
                lambda a, own: lax.dynamic_index_in_dim(a, source, 0, False).astype(own.dtype),
                gathered,
                array,
            ),
        )

    return lax.fori_loop(0, ahead, one, state)


def quantize(weight, channel_scale):
    ratios = weight.astype(jnp.float32) / channel_scale
    clipped = jnp.clip(ratios, -QMAX, QMAX)
    levels = jnp.floor(clipped + 0.5)
    inside = jnp.abs(ratios) <= QMAX
    slopes = jnp.where(inside, levels - ratios, levels)
    return (levels, slopes, inside.astype(jnp.float32))


def stretch_terms(decay_logs, inputs_f, outputs_f):
    cumul = jnp.cumsum(decay_logs, axis=0)
    ending = cumul[-1]
    spread = cumul[:, None, :] - cumul[None, :, :]
    length = decay_logs.shape[0]
    causal = jnp.arange(length)[:, None] >= jnp.arange(length)[None, :]
    mixing = jnp.exp(jnp.where(causal[:, :, None], spread, -jnp.inf))
    intersection = jnp.dot(outputs_f, inputs_f.T, precision=precise)
    return (cumul, ending, mixing * intersection[:, :, None])


def forward_step(carried, pieces):
    values, cumul, ending, weights, inputs_f, outputs_f = pieces
    inner = jnp.einsum("sth,thp->shp", weights, values, precision=precise)
    outer = jnp.exp(cumul)[:, :, None] * jnp.einsum(
        "sn,hnp->shp", outputs_f, carried, precision=precise
    )
    fresh = jnp.einsum(
        "th,tn,thp->hnp", jnp.exp(ending[None, :] - cumul), inputs_f, values, precision=precise
    )
    return (jnp.exp(ending)[:, None, None] * carried + fresh, inner + outer)


def backward_step(carried, pieces):
    grads, cumul, ending, weights, inputs_f, outputs_f = pieces
    inner = jnp.einsum("sth,shp->thp", weights, grads, precision=precise)
    outer = jnp.exp(ending[None, :] - cumul)[:, :, None] * jnp.einsum(
        "tn,hnp->thp", inputs_f, carried, precision=precise
    )
    fresh = jnp.einsum("sh,sn,shp->hnp", jnp.exp(cumul), outputs_f, grads, precision=precise)
    return (jnp.exp(ending)[:, None, None] * carried + fresh, inner + outer)


def join_forward(earlier, later):
    return (earlier[0] * later[0], later[0][:, None, None] * earlier[1] + later[1])


def join_backward(earlier, later):
    return (earlier[0] * later[0], later[1] + later[0][:, None, None] * earlier[1])


def per_device(
    tokens, grad_out, in_weight, in_scale, out_weight, out_scale, state_in, state_out, log_decay
):
    local_rows = tokens.shape[0]
    heads_here = log_decay.shape[1]
    width_here = in_scale.shape[0]
    head_size = width_here // heads_here
    state_size = state_in.shape[1]
    weight_rows = in_weight.shape[0]
    blocks = local_rows // STRETCH
    row_start = lax.axis_index("seq") * weight_rows
    out_scale_rows = lax.dynamic_slice_in_dim(out_scale, row_start, weight_rows)
    in_levels, in_slopes, in_inside = quantize(in_weight, in_scale[None, :])
    out_levels, out_slopes, out_inside = quantize(out_weight, out_scale_rows[:, None])
    in_codes = lax.all_gather(in_levels.astype(jnp.bfloat16), "seq", axis=0, tiled=True)
    out_codes = lax.all_gather(out_levels.astype(jnp.bfloat16), "seq", axis=0, tiled=True)
    features = lax.all_gather(tokens, "tp", axis=1, tiled=True)
    cotangent = lax.all_gather(grad_out, "tp", axis=1, tiled=True)
    projected = jnp.dot(features, in_codes, preferred_element_type=jnp.float32) * in_scale[None, :]
    scaled_grad = (cotangent.astype(jnp.float32) * out_scale[None, :]).astype(jnp.bfloat16)
    grad_mixed = jnp.dot(scaled_grad, out_codes, preferred_element_type=jnp.float32)
    inputs_full = state_in.astype(jnp.float32)
    outputs_full = state_out.astype(jnp.float32)
    decay_blocks = log_decay.reshape(blocks, STRETCH, heads_here)
    input_blocks = inputs_full.reshape(blocks, STRETCH, state_size)
    output_blocks = outputs_full.reshape(blocks, STRETCH, state_size)
    cumul, ending, weights = jax.vmap(stretch_terms)(decay_blocks, input_blocks, output_blocks)
    value_blocks = projected.reshape(blocks, STRETCH, heads_here, head_size)
    grad_blocks = grad_mixed.reshape(blocks, STRETCH, heads_here, head_size)
    empty = jnp.zeros((heads_here, state_size, head_size), jnp.float32)
    local_state, mixed_local = lax.scan(
        forward_step, empty, (value_blocks, cumul, ending, weights, input_blocks, output_blocks)
    )
    local_grad_state, grad_local = lax.scan(
        backward_step,
        empty,
        (grad_blocks, cumul, ending, weights, input_blocks, output_blocks),
        reverse=True,
    )
    running = jnp.cumsum(log_decay, axis=0)
    device_total = running[-1]
    device_decay = jnp.exp(device_total)
    identity = (jnp.ones_like(device_decay), empty)
    entering = prefix((device_decay, local_state), "seq", join_forward, identity, False)[1]
    leaving = prefix((device_decay, local_grad_state), "seq", join_backward, identity, True)[1]
    mixed = mixed_local.reshape(local_rows, heads_here, head_size) + jnp.exp(running)[
        :, :, None
    ] * jnp.einsum("tn,hnp->thp", outputs_full, entering, precision=precise)
    grad_values = grad_local.reshape(local_rows, heads_here, head_size) + jnp.exp(
        device_total[None, :] - running
    )[:, :, None] * jnp.einsum("tn,hnp->thp", inputs_full, leaving, precision=precise)
    mixed = mixed.reshape(local_rows, width_here)
    grad_values = grad_values.reshape(local_rows, width_here)
    mixed_b = mixed.astype(jnp.bfloat16)
    grad_b = grad_values.astype(jnp.bfloat16)
    grad_scaled = (grad_values * in_scale[None, :]).astype(jnp.bfloat16)
    piece = features
    in_total = lax.psum_scatter(
        jnp.einsum("td,tc->dc", piece, grad_b, preferred_element_type=jnp.float32).astype(
            jnp.bfloat16
        ),
        "seq",
        scatter_dimension=0,
        tiled=True,
    ).astype(jnp.float32)
    piece = cotangent
    out_total = lax.psum_scatter(
        jnp.einsum("td,tc->dc", piece, mixed_b, preferred_element_type=jnp.float32).astype(
            jnp.bfloat16
        ),
        "seq",
        scatter_dimension=0,
        tiled=True,
    ).astype(jnp.float32)
    partial_tokens = jnp.einsum(
        "tc,dc->td", grad_scaled, in_codes, preferred_element_type=jnp.float32
    )
    grad_tokens = lax.psum_scatter(
        partial_tokens.astype(jnp.bfloat16), "tp", scatter_dimension=1, tiled=True
    )
    in_part = jnp.sum(in_total * in_slopes, axis=0)
    out_part = jnp.sum(out_total * out_slopes, axis=1)
    in_sum = lax.psum(in_part, "seq")
    out_sum = lax.psum(out_part, "tp")
    grad_in_scale = in_sum / jnp.sqrt(jnp.float32(D * QMAX))
    grad_out_scale = out_sum / jnp.sqrt(jnp.float32(HEADS * HEAD_DIM * QMAX))
    return (
        grad_tokens,
        in_total * in_inside,
        grad_in_scale,
        out_total * out_inside,
        grad_out_scale,
    )


def solution(mesh):
    placed = (
        P("seq", "tp"),
        P("seq", "tp"),
        P("seq", "tp"),
        P("tp"),
        P("seq", "tp"),
        P(),
        P("seq", None),
        P("seq", None),
        P("seq", "tp"),
    )
    return jax.shard_map(
        per_device,
        mesh=mesh,
        in_specs=placed,
        out_specs=(P("seq", "tp"), P("seq", "tp"), P("tp"), P("seq", "tp"), P("seq")),
        check_vma=False,
    )
```

profile of v0, /device:TPU:6, one launch (start us, length us, event | category | flops | bytes accessed | tf_op | source)
XLA Modules:
  0.0 612.6 jit_solution(15400213899961906926)
XLA Ops:
  10.5 1.3 reduce-window.14
  12.4 41.5 %all-gather.10.cloned.1.call-done = bf16[256,4096]{1,0:T(8,128)(2,1)} async-done(((bf16[256,512]{1,0:T(8,128)(2,1)}), bf16[256,4096]{1,0:T(8,128)(2,1)}) %all-gather.10.cloned.1.call-update) | async-done | bytes 2097168 | tf_op jit(solution)/shard_map/all_gather | solution.py:104
  53.9 55.4 %all-gather.12.cloned.1.call-done = bf16[4096,512]{0,1:T(8,128)(2,1)} async-done(((bf16[128,512]{0,1:T(8,128)(2,1)}), bf16[4096,512]{0,1:T(8,128)(2,1)}) %all-gather.12.cloned.1.call-update) | async-done | bytes 4194320 | tf_op jit(solution)/shard_map/all_gather | solution.py:102
  109.3 4.1 fusion.2
  116.2 18.9 %all-gather.2 = bf16[32,1,8]{2,1,0:T(2,128)(2,1)S(1)} all-gather(bf16[1,1,8]{2,1,0:T(2,128)(2,1)S(1)} %bitcast.154), channel_id=1, replica_groups=mesh['seq'=32,'tp'=8] {'seq'}, dimensions={0}, use_global_device_ids=true | all-gather | bytes 528 | tf_op jit(solution)/shard_map/all_gather | solution.py:19
  135.6 1.8 fusion.6
  137.5 28.1 %all-gather.18.cloned.1.call-done = bf16[256,128,64]{1,2,0:T(8,128)(2,1)} async-done(((bf16[8,128,64]{1,2,0:T(8,128)(2,1)}), bf16[256,128,64]{1,2,0:T(8,128)(2,1)}) %all-gather.18.cloned.1.call-update) | async-done | bytes 4194320 | tf_op jit(solution)/shard_map/all_gather | solution.py:19
  165.6 32.6 %while.16 = (s32[]{:T(128)}, f32[8,128,64]{2,1,0:T(8,128)S(1)}, s32[]{:T(128)}, bf16[32,8,128,64]{2,3,1,0:T(8,128)(2,1)}, bf16[32,8]{1,0:T(8,128)(2,1)S(1)}, /*index=5*/s32[]{:T(128)}, s32[]{:T(128)}, s32[]{:T(128)}, s32[]{:T(128)}) while((s32[]{:T(128)}, f32[8,128,64]{2,1,0:T(8,128)S(1)}, s32[]{:T(128)}, bf16[32,8,128,64]{2,3,1,0:T(8,128)(2,1)}, ...), condition=%wide.region_5.6_spmd, body=%wide.region_4.5_spmd.sunk | while | flops 196622 | bytes 1179883 | solution.py:34
  199.3 8.6 %all-gather.16.cloned.1.call-done = bf16[256,4096]{1,0:T(8,128)(2,1)} async-done(((bf16[256,512]{1,0:T(8,128)(2,1)}), bf16[256,4096]{1,0:T(8,128)(2,1)}) %all-gather.16.cloned.1.call-update) | async-done | bytes 2097168 | tf_op jit(solution)/shard_map/all_gather | solution.py:103
  207.9 4.8 fusion
  212.7 6.5 %copy.81 = bf16[4096,512]{1,0:T(8,128)(2,1)} copy(bf16[4096,512]{0,1:T(8,128)(2,1)} %fusion) | data formatting | bytes 8388608
  220.2 87.2 %reduce-scatter.10.cloned.1.call-done = bf16[128,512]{1,0:T(8,128)(2,1)} async-done(((bf16[4096,512]{1,0:T(8,128)(2,1)}), bf16[128,512]{1,0:T(8,128)(2,1)}) %reduce-scatter.10.cloned.1.call-update) | async-done | bytes 131088
  309.3 54.8 %all-gather.14.cloned.1.call-done = bf16[4096,512]{0,1:T(8,128)(2,1)} async-done(((bf16[128,512]{0,1:T(8,128)(2,1)}), bf16[4096,512]{0,1:T(8,128)(2,1)}) %all-gather.14.cloned.1.call-update) | async-done | bytes 4194320 | tf_op jit(solution)/shard_map/all_gather | solution.py:101
  364.1 3.5 convolution_multiply_fusion
  369.6 3.5 fusion.7
  373.0 47.4 %all-gather.20.cloned.1.call-done = bf16[256,128,64]{1,2,0:T(8,128)(2,1)} async-done(((bf16[8,128,64]{1,2,0:T(8,128)(2,1)}), bf16[256,128,64]{1,2,0:T(8,128)(2,1)}) %all-gather.20.cloned.1.call-update) | async-done | bytes 4194320 | tf_op jit(solution)/shard_map/all_gather | solution.py:19
  420.5 8.0 %while.17 = (s32[]{:T(128)}, f32[8,128,64]{2,1,0:T(8,128)S(1)}, s32[]{:T(128)}, bf16[32,8]{1,0:T(8,128)(2,1)S(1)}, bf16[32,8,128,64]{2,3,1,0:T(8,128)(2,1)}, /*index=5*/s32[]{:T(128)}, s32[]{:T(128)}, s32[]{:T(128)}) while((s32[]{:T(128)}, f32[8,128,64]{2,1,0:T(8,128)S(1)}, s32[]{:T(128)}, bf16[32,8]{1,0:T(8,128)(2,1)S(1)}, ...), condition=%wide.region_11.12_spmd, body=%wide.region_10.11_spmd.sunk | while | flops 196621 | bytes 1179863 | solution.py:34
  430.1 3.2 fusion.1
  433.4 6.5 %copy.83 = bf16[4096,512]{1,0:T(8,128)(2,1)} copy(bf16[4096,512]{0,1:T(8,128)(2,1)} %fusion.1) | data formatting | bytes 8388608
  440.1 4.9 convolution_convert_fusion.2
  445.8 83.4 %psum.14 = f32[512]{0:T(512)S(1)} all-reduce(f32[512]{0:T(512)S(1)} %get-tuple-element.273), channel_id=1, replica_groups=mesh['seq'=32,'tp'=8] {'seq'}, use_global_device_ids=true, to_apply=%region_9.10 | all-reduce | flops 512 | bytes 4096 | tf_op jit(solution)/shard_map/psum | solution.py:169
  529.8 31.0 %reduce-scatter.12.cloned.1.call-done = bf16[128,512]{1,0:T(8,128)(2,1)} async-done(((bf16[4096,512]{1,0:T(8,128)(2,1)}), bf16[128,512]{1,0:T(8,128)(2,1)}) %reduce-scatter.12.cloned.1.call-update) | async-done | bytes 131088
  562.8 17.4 %psum.15 = f32[128]{0:T(128)S(1)} all-reduce(f32[128]{0:T(128)S(1)} %get-tuple-element.275), channel_id=1, replica_groups=mesh['seq'=32,'tp'=8] {'tp'}, use_global_device_ids=true, to_apply=%region_14.15 | all-reduce | flops 128 | bytes 1024 | tf_op jit(solution)/shard_map/psum | solution.py:170
  580.7 25.3 %reduce-scatter.8.cloned.1.call-done = bf16[256,512]{1,0:T(8,128)(2,1)} async-done(((bf16[256,4096]{1,0:T(8,128)(2,1)}), bf16[256,512]{1,0:T(8,128)(2,1)}) %reduce-scatter.8.cloned.1.call-update) | async-done | bytes 262160 | tf_op jit(solution)/shard_map/reduce_scatter | solution.py:164
  (203 shorter events, 58.0 us)
Async XLA Ops:
  7.2 128.3 %copy-start = (bf16[256,128]{1,0:T(8,128)(2,1)S(1)}, bf16[256,128]{1,0:T(8,128)(2,1)}, u32[]{:S(2)}) copy-start(bf16[256,128]{1,0:T(8,128)(2,1)} %param.19) | copy-start | bytes 196612
  7.2 46.7 %all-gather.10.cloned.1.call-start = ((), (), s32[]{:S(2)}) async-start(), calls=%async_computation.3 | async-start | bytes 2359296 | tf_op jit(solution)/shard_map/all_gather | solution.py:104
  7.9 101.4 %all-gather.12.cloned.1.call-start = ((), (), s32[]{:S(2)}) async-start(), calls=%async_computation.4 | async-start | bytes 4325376 | tf_op jit(solution)/shard_map/all_gather | solution.py:102
  10.5 155.0 %all-gather.18.cloned.1.call-start = ((), (), s32[]{:S(2)}) async-start(), calls=%async_computation.8 | async-start | bytes 4325376 | tf_op jit(solution)/shard_map/all_gather | solution.py:19
  12.4 101.1 %copy-start.3 = (bf16[256,128]{1,0:T(8,128)(2,1)S(1)}, bf16[256,128]{1,0:T(8,128)(2,1)}, u32[]{:S(2)}) copy-start(bf16[256,128]{1,0:T(8,128)(2,1)} %param.20) | copy-start | bytes 196612
  12.4 102.8 %copy-start.8 = (f32[256,8]{0,1:T(8,128)S(1)}, f32[256,8]{0,1:T(8,128)}, u32[]{:S(2)}) copy-start(f32[256,8]{0,1:T(8,128)} %param.21) | copy-start | bytes 24580
  114.5 93.4 %all-gather.16.cloned.1.call-start = ((), (), s32[]{:S(2)}) async-start(), calls=%async_computation.7 | async-start | bytes 2359296 | tf_op jit(solution)/shard_map/all_gather | solution.py:103
  115.1 192.3 %reduce-scatter.10.cloned.1.call-start = ((), (), s32[]{:S(2)}) async-start(), calls=%async_computation.10 | async-start | bytes 4325376
  135.6 30.0 %copy-start.5 = (f32[256,256]{1,0:T(8,128)}, f32[256,256]{1,0:T(8,128)S(1)}, u32[]{:S(2)}) copy-start(f32[256,256]{1,0:T(8,128)S(1)} %fusion.57) | copy-start | bytes 786436
  219.2 0.9 copy-start.7
  219.2 89.2 %copy-start.9 = (f32[512]{0:T(512)S(1)}, f32[512]{0:T(512)}, u32[]{:S(2)}) copy-start(f32[512]{0:T(512)} %param.16) | copy-start | bytes 6148
  219.2 145.0 %copy-start.2 = (bf16[256,4096]{1,0:T(8,128)(2,1)S(1)}, bf16[256,4096]{1,0:T(8,128)(2,1)}, u32[]{:S(2)}) copy-start(bf16[256,4096]{1,0:T(8,128)(2,1)} %all-gather.16.cloned.1.call-done) | copy-start | bytes 6291460
  219.2 145.0 %all-gather.14.cloned.1.call-start = ((), (), s32[]{:S(2)}) async-start(), calls=%async_computation.5 | async-start | bytes 4325376 | tf_op jit(solution)/shard_map/all_gather | solution.py:101
  309.3 60.3 %copy-start.6 = (f32[256,256]{1,0:T(8,128)S(1)}, f32[256,256]{1,0:T(8,128)}, u32[]{:S(2)}) copy-start(f32[256,256]{1,0:T(8,128)} %copy-done.5) | copy-start | bytes 786436
  309.3 111.2 %all-gather.20.cloned.1.call-start = ((), (), s32[]{:S(2)}) async-start(), calls=%async_computation.9 | async-start | bytes 4325376 | tf_op jit(solution)/shard_map/all_gather | solution.py:19
  367.6 0.8 copy-start.4
  369.5 191.3 %reduce-scatter.12.cloned.1.call-start = ((), (), s32[]{:S(2)}) async-start(), calls=%async_computation.11 | async-start | bytes 4325376
  428.5 1.6 copy-start.1
  439.9 166.1 %reduce-scatter.8.cloned.1.call-start = ((), (), s32[]{:S(2)}) async-start(), calls=%async_computation.6 | async-start | bytes 2359296 | tf_op jit(solution)/shard_map/reduce_scatter | solution.py:164
Sparse Core Ops, SparseCore 0:
  9.8 44.0 all-gather.9
  56.9 52.3 all-gather.11
  114.6 50.8 all-gather.17
  167.2 40.6 all-gather.15
  219.3 88.0 reduce-scatter.9
  310.6 53.5 all-gather.13
  369.6 50.7 all-gather.19
  440.0 120.7 reduce-scatter.11
  563.9 42.0 reduce-scatter.7
where the time goes:
time: 614 us; the launch traced here: 613 us
  waiting for transfers between devices  381 us (62%)
  blocking collectives  120 us (20%)
  local copies, waits for them, and re-layouts  55.6 us (9%)
  matrix products  30.2 us (5%)
  between operations  14.1 us (2%)
  other arithmetic  10.6 us (2%)
    unnamed x11, waiting for transfers between devices  119 us
    psum x1, blocking collectives, per_device(): in_sum = lax.psum(in_part, 'seq')  83.4 us
    all_gather x2, waiting for transfers between devices, prefix(): lax.all_gather(a.astype(kind), axis)  75.5 us
    all_gather x1, waiting for transfers between devices, per_device(): lax.all_gather(out_levels.astype(jnp.bfloat16), 'seq', axis=0, tiled=True)  55.4 us
    all_gather x1, waiting for transfers between devices, per_device(): lax.all_gather(in_levels.astype(jnp.bfloat16), 'seq', axis=0, tiled=True)  54.8 us
    all_gather x1, waiting for transfers between devices, per_device(): cotangent = lax.all_gather(grad_out, 'tp', axis=1, tiled=True)  41.5 us
    dynamic_slice x62, local copies, waits for them, and re-layouts, one(): lax.dynamic_index_in_dim(a, source, 0, False).astype(own.dtype)  34 us
    reduce_scatter x1, waiting for transfers between devices, per_device(): lax.psum_scatter(partial_tokens.astype(jnp.bfloat16), 'tp', scatter_dimen...  25.3 us
  transfers between devices with their start and end apart: 9, of which 9 were waited for; matrix products, arithmetic and copies ran while one was open for 9% of the time, Pallas kernels for 0%

commit v1 on v0

--- a/solution.py
+++ b/solution.py
@@ -1,3 +1,4 @@
+import functools
 import jax
 import jax.numpy as jnp
 from jax import lax
@@ -9,6 +10,36 @@
 STRETCH = 256
 QMAX = 7
 precise = lax.Precision.HIGHEST
+
+
+def post_the_task(packet, shard_axis):
+    axis_len = lax.axis_size(shard_axis)
+    chunks = []
+    to_i = 0
+    while to_i < axis_len:
+        chunks.append((to_i, (to_i + 1) % axis_len))
+        to_i += 1
+    rows = []
+    to_i = 0
+    while to_i < axis_len:
+        rows.append((to_i, (to_i - 1) % axis_len))
+        to_i += 1
+    small, all_rows = ([packet], [packet])
+    for _ in range(axis_len // 2):
+        shaped = lax.ppermute(small[-1], axis_name=shard_axis, perm=chunks)
+        small.append(shaped)
+    dev_j = 0
+    while dev_j < (axis_len - 1) // 2:
+        long_array = lax.ppermute(all_rows[-1], shard_axis, perm=rows)
+        all_rows.append(long_array)
+        dev_j += 1
+    w1 = jnp.concatenate([*small[::-1], *all_rows[1:]], 1)
+    local_part = lax.axis_index(shard_axis)
+    main = jnp.roll(w1, (local_part - axis_len // 2) * packet.shape[1], 1)
+    return main
+
+
+raise_local_data = functools.partial(post_the_task, shard_axis="tp")
 
 
 def prefix(array, axis, join, neutral, backward):
@@ -101,7 +132,7 @@
     in_codes = lax.all_gather(in_levels.astype(jnp.bfloat16), "seq", axis=0, tiled=True)
     out_codes = lax.all_gather(out_levels.astype(jnp.bfloat16), "seq", axis=0, tiled=True)
     features = lax.all_gather(tokens, "tp", axis=1, tiled=True)
-    cotangent = lax.all_gather(grad_out, "tp", axis=1, tiled=True)
+    cotangent = raise_local_data(grad_out)
     projected = jnp.dot(features, in_codes, preferred_element_type=jnp.float32) * in_scale[None, :]
     scaled_grad = (cotangent.astype(jnp.float32) * out_scale[None, :]).astype(jnp.bfloat16)
     grad_mixed = jnp.dot(scaled_grad, out_codes, preferred_element_type=jnp.float32)

time: 614 us -> 567 us (0.923)
  waiting for transfers between devices: 381 us -> 313 us
  starting transfers between devices: 0.37 us -> 13 us
  local copies, waits for them, and re-layouts: 55.6 us -> 62.3 us
    all_gather x1, waiting for transfers between devices: 55.4 us -> 8.25 us  [per_device(): lax.all_gather(out_levels.astype(jnp.bfloat16), 'seq', axis=0, tiled=True)]
    all_gather x1 -> x0, waiting for transfers between devices: 41.5 us -> none  [per_device(): cotangent = lax.all_gather(grad_out, 'tp', axis=1, tiled=True)]
    ppermute x0 -> x7, waiting for transfers between devices: none -> 22.1 us  [the longest x4 22.1 us: post_the_task(): shaped = lax.ppermute(small[-1], axis_name=shard_axis, perm=chunks)]
    ppermute x0 -> x7, starting transfers between devices: none -> 12.7 us  [the longest x3 10.6 us: post_the_task(): long_array = lax.ppermute(all_rows[-1], shard_axis, perm=rows)]
    unnamed x28 -> x44, local copies, waits for them, and re-layouts: 20.1 us -> 26 us
    unnamed x11 -> x10, waiting for transfers between devices: 119 us -> 119 us
  transfers between devices with their start and end apart: 9 -> 15, of which waited for: 9 -> 12; matrix products, arithmetic and copies ran while one was open for 9% -> 11% of each run, Pallas kernels for 0% -> 0%
where the time goes in v1:
time: 567 us; the launch traced here: 566 us
  waiting for transfers between devices  313 us (55%)
  blocking collectives  120 us (21%)
  local copies, waits for them, and re-layouts  62.3 us (11%)
  matrix products  31.8 us (6%)
  between operations  14.4 us (3%)
  starting transfers between devices  13 us (2%)
  other arithmetic  10.6 us (2%)
    unnamed x10, waiting for transfers between devices  119 us
    psum x1, blocking collectives, per_device(): in_sum = lax.psum(in_part, 'seq')  83.4 us
    all_gather x2, waiting for transfers between devices, prefix(): lax.all_gather(a.astype(kind), axis)  74.6 us
    all_gather x1, waiting for transfers between devices, per_device(): lax.all_gather(in_levels.astype(jnp.bfloat16), 'seq', axis=0, tiled=True)  54.8 us
    dynamic_slice x62, local copies, waits for them, and re-layouts, one(): lax.dynamic_index_in_dim(a, source, 0, False).astype(own.dtype)  34 us
    unnamed x44, local copies, waits for them, and re-layouts  26 us
    reduce_scatter x1, waiting for transfers between devices, per_device(): lax.psum_scatter(partial_tokens.astype(jnp.bfloat16), 'tp', scatter_dimen...  25 us
    ppermute x4, waiting for transfers between devices, post_the_task(): shaped = lax.ppermute(small[-1], axis_name=shard_axis, perm=chunks)  22.1 us
  transfers between devices with their start and end apart: 15, of which 12 were waited for; matrix products, arithmetic and copies ran while one was open for 11% of the time, Pallas kernels for 0%

profile of v1, /device:TPU:6, one launch (start us, length us, event | category | flops | bytes accessed | tf_op | source)
XLA Modules:
  0.0 565.9 jit_solution(11866043661672841887)
XLA Ops:
  11.9 4.0 collective-permute-start.4
  17.1 5.2 collective-permute-done
  22.5 8.5 %collective-permute-done.1 = bf16[256,512]{1,0:T(8,128)(2,1)S(1)} collective-permute-done((bf16[256,512]{1,0:T(8,128)(2,1)S(1)}, bf16[256,512]{1,0:T(8,128)(2,1)S(1)}, u32[]{:S(2)}, u32[]{:S(2)}) %collective-permute-start.1) | collective-permute-done | bytes 262176 | tf_op jit(solution)/shard_map/ppermute | solution.py:29
  34.6 4.3 collective-permute-done.2
  42.4 4.1 collective-permute-done.3
  59.5 8.3 %all-gather.9.cloned.1.call-done = bf16[4096,512]{0,1:T(8,128)(2,1)} async-done(((bf16[128,512]{0,1:T(8,128)(2,1)}), bf16[4096,512]{0,1:T(8,128)(2,1)}) %all-gather.9.cloned.1.call-update) | async-done | bytes 4194320 | tf_op jit(solution)/shard_map/all_gather | solution.py:133
  67.8 4.1 fusion.1
  74.9 18.9 %all-gather.2 = bf16[32,1,8]{2,1,0:T(2,128)(2,1)S(1)} all-gather(bf16[1,1,8]{2,1,0:T(2,128)(2,1)S(1)} %bitcast.151), channel_id=1, replica_groups=mesh['seq'=32,'tp'=8] {'seq'}, dimensions={0}, use_global_device_ids=true | all-gather | bytes 528 | tf_op jit(solution)/shard_map/all_gather | solution.py:50
  96.8 27.2 %all-gather.15.cloned.1.call-done = bf16[256,128,64]{1,2,0:T(8,128)(2,1)} async-done(((bf16[8,128,64]{1,2,0:T(8,128)(2,1)}), bf16[256,128,64]{1,2,0:T(8,128)(2,1)}) %all-gather.15.cloned.1.call-update) | async-done | bytes 4194320 | tf_op jit(solution)/shard_map/all_gather | solution.py:50
  124.0 32.8 %while.16 = (s32[]{:T(128)}, f32[8,128,64]{2,1,0:T(8,128)S(1)}, s32[]{:T(128)}, bf16[32,8,128,64]{2,3,1,0:T(8,128)(2,1)}, bf16[32,8]{1,0:T(8,128)(2,1)S(1)}, /*index=5*/s32[]{:T(128)}, s32[]{:T(128)}, s32[]{:T(128)}, s32[]{:T(128)}) while((s32[]{:T(128)}, f32[8,128,64]{2,1,0:T(8,128)S(1)}, s32[]{:T(128)}, bf16[32,8,128,64]{2,3,1,0:T(8,128)(2,1)}, ...), condition=%wide.region_5.6_spmd, body=%wide.region_4.5_spmd.sunk | while | flops 196622 | bytes 1179883 | solution.py:65
  157.9 8.8 %all-gather.13.cloned.1.call-done = bf16[256,4096]{1,0:T(8,128)(2,1)} async-done(((bf16[256,512]{1,0:T(8,128)(2,1)}), bf16[256,4096]{1,0:T(8,128)(2,1)}) %all-gather.13.cloned.1.call-update) | async-done | bytes 2097168 | tf_op jit(solution)/shard_map/all_gather | solution.py:134
  166.8 4.8 fusion
  171.6 6.5 %copy.85 = bf16[4096,512]{1,0:T(8,128)(2,1)} copy(bf16[4096,512]{0,1:T(8,128)(2,1)} %fusion) | data formatting | bytes 8388608
  179.1 87.2 %reduce-scatter.10.cloned.1.call-done = bf16[128,512]{1,0:T(8,128)(2,1)} async-done(((bf16[4096,512]{1,0:T(8,128)(2,1)}), bf16[128,512]{1,0:T(8,128)(2,1)}) %reduce-scatter.10.cloned.1.call-update) | async-done | bytes 131088
  268.3 54.8 %all-gather.11.cloned.1.call-done = bf16[4096,512]{0,1:T(8,128)(2,1)} async-done(((bf16[128,512]{0,1:T(8,128)(2,1)}), bf16[4096,512]{0,1:T(8,128)(2,1)}) %all-gather.11.cloned.1.call-update) | async-done | bytes 4194320 | tf_op jit(solution)/shard_map/all_gather | solution.py:132
  323.1 3.5 convolution_multiply_fusion
  332.0 47.4 %all-gather.17.cloned.1.call-done = bf16[256,128,64]{1,2,0:T(8,128)(2,1)} async-done(((bf16[8,128,64]{1,2,0:T(8,128)(2,1)}), bf16[256,128,64]{1,2,0:T(8,128)(2,1)}) %all-gather.17.cloned.1.call-update) | async-done | bytes 4194320 | tf_op jit(solution)/shard_map/all_gather | solution.py:50
  379.4 7.8 %while.17 = (s32[]{:T(128)}, f32[8,128,64]{2,1,0:T(8,128)S(1)}, s32[]{:T(128)}, bf16[32,8]{1,0:T(8,128)(2,1)S(1)}, bf16[32,8,128,64]{2,3,1,0:T(8,128)(2,1)}, /*index=5*/s32[]{:T(128)}, s32[]{:T(128)}, s32[]{:T(128)}) while((s32[]{:T(128)}, f32[8,128,64]{2,1,0:T(8,128)S(1)}, s32[]{:T(128)}, bf16[32,8]{1,0:T(8,128)(2,1)S(1)}, ...), condition=%wide.region_11.12_spmd, body=%wide.region_10.11_spmd.sunk | while | flops 196621 | bytes 1179863 | solution.py:65
  388.3 4.9 convolution_convert_fusion
  393.4 4.9 convolution_convert_fusion.2
  399.1 83.4 %psum.14 = f32[512]{0:T(512)S(1)} all-reduce(f32[512]{0:T(512)S(1)} %get-tuple-element.273), channel_id=1, replica_groups=mesh['seq'=32,'tp'=8] {'seq'}, use_global_device_ids=true, to_apply=%region_9.10 | all-reduce | flops 512 | bytes 4096 | tf_op jit(solution)/shard_map/psum | solution.py:200
  483.1 31.0 %reduce-scatter.12.cloned.1.call-done = bf16[128,512]{1,0:T(8,128)(2,1)} async-done(((bf16[4096,512]{1,0:T(8,128)(2,1)}), bf16[128,512]{1,0:T(8,128)(2,1)}) %reduce-scatter.12.cloned.1.call-update) | async-done | bytes 131088
  516.1 17.4 %psum.15 = f32[128]{0:T(128)S(1)} all-reduce(f32[128]{0:T(128)S(1)} %get-tuple-element.275), channel_id=1, replica_groups=mesh['seq'=32,'tp'=8] {'tp'}, use_global_device_ids=true, to_apply=%region_14.15 | all-reduce | flops 128 | bytes 1024 | tf_op jit(solution)/shard_map/psum | solution.py:201
  534.0 25.0 %reduce-scatter.8.cloned.1.call-done = bf16[256,512]{1,0:T(8,128)(2,1)} async-done(((bf16[256,4096]{1,0:T(8,128)(2,1)}), bf16[256,512]{1,0:T(8,128)(2,1)}) %reduce-scatter.8.cloned.1.call-update) | async-done | bytes 262160 | tf_op jit(solution)/shard_map/reduce_scatter | solution.py:195
  (231 shorter events, 85.8 us)
Async XLA Ops:
  7.2 86.9 %copy-start = (bf16[256,128]{1,0:T(8,128)(2,1)S(1)}, bf16[256,128]{1,0:T(8,128)(2,1)}, u32[]{:S(2)}) copy-start(bf16[256,128]{1,0:T(8,128)(2,1)} %param.19) | copy-start | bytes 196612
  7.2 49.3 %copy-start.2 = (bf16[256,512]{1,0:T(8,128)(2,1)S(1)}, bf16[256,512]{1,0:T(8,128)(2,1)}, u32[]{:S(2)}) copy-start(bf16[256,512]{1,0:T(8,128)(2,1)} %param.14) | copy-start | bytes 786436
  7.2 60.6 %all-gather.9.cloned.1.call-start = ((), (), s32[]{:S(2)}) async-start(), calls=%async_computation.3 | async-start | bytes 4325376 | tf_op jit(solution)/shard_map/all_gather | solution.py:133
  9.8 114.2 %all-gather.15.cloned.1.call-start = ((), (), s32[]{:S(2)}) async-start(), calls=%async_computation.7 | async-start | bytes 4325376 | tf_op jit(solution)/shard_map/all_gather | solution.py:50
  9.9 12.5 %collective-permute-start = (bf16[256,512]{1,0:T(8,128)(2,1)}, bf16[256,512]{1,0:T(8,128)(2,1)S(1)}, u32[]{:S(2)}, u32[]{:S(2)}) collective-permute-start(bf16[256,512]{1,0:T(8,128)(2,1)} %param.14), channel_id=1, source_target_pairs={{0,1},{1,2},{2,3},{3,4},{4,5},{5,6},{6,7},{7,0},{8,9},{9,10},{10,1... | collective-permute-start | bytes 786440 | tf_op jit(solution)/shard_map/ppermute | solution.py:29
  11.9 19.4 %collective-permute-start.4 = (bf16[256,512]{1,0:T(8,128)(2,1)}, bf16[256,512]{1,0:T(8,128)(2,1)S(1)}, u32[]{:S(2)}, u32[]{:S(2)}) collective-permute-start(bf16[256,512]{1,0:T(8,128)(2,1)} %param.14), channel_id=1, source_target_pairs={{0,7},{1,0},{2,1},{3,2},{4,3},{5,4},{6,5},{7,6},{8,15},{9,8},{10,9... | collective-permute-start | bytes 786440 | tf_op jit(solution)/shard_map/ppermute | solution.py:33
  22.3 8.7 %collective-permute-start.1 = (bf16[256,512]{1,0:T(8,128)(2,1)S(1)}, bf16[256,512]{1,0:T(8,128)(2,1)S(1)}, u32[]{:S(2)}, u32[]{:S(2)}) collective-permute-start(bf16[256,512]{1,0:T(8,128)(2,1)S(1)} %collective-permute-done), channel_id=1, source_target_pairs={{0,1},{1,2},{2,3},{3,4},{4,5},{5,6},{6,7},{7,0},{8,9},{9,10},{10,1... | collective-permute-start | bytes 786440 | tf_op jit(solution)/shard_map/ppermute | solution.py:29
  31.0 7.9 %collective-permute-start.2 = (bf16[256,512]{1,0:T(8,128)(2,1)S(1)}, bf16[256,512]{1,0:T(8,128)(2,1)S(1)}, u32[]{:S(2)}, u32[]{:S(2)}) collective-permute-start(bf16[256,512]{1,0:T(8,128)(2,1)S(1)} %collective-permute-done.1), channel_id=1, source_target_pairs={{0,1},{1,2},{2,3},{3,4},{4,5},{5,6},{6,7},{7,0},{8,9},{9,10},{10,1... | collective-permute-start | bytes 786440 | tf_op jit(solution)/shard_map/ppermute | solution.py:29
  31.3 7.7 %collective-permute-start.5 = (bf16[256,512]{1,0:T(8,128)(2,1)S(1)}, bf16[256,512]{1,0:T(8,128)(2,1)S(1)}, u32[]{:S(2)}, u32[]{:S(2)}) collective-permute-start(bf16[256,512]{1,0:T(8,128)(2,1)S(1)} %collective-permute-done.4), channel_id=1, source_target_pairs={{0,7},{1,0},{2,1},{3,2},{4,3},{5,4},{6,5},{7,6},{8,15},{9,8},{10,9... | collective-permute-start | bytes 786440 | tf_op jit(solution)/shard_map/ppermute | solution.py:33
  38.9 7.6 %collective-permute-start.3 = (bf16[256,512]{1,0:T(8,128)(2,1)S(1)}, bf16[256,512]{1,0:T(8,128)(2,1)S(1)}, u32[]{:S(2)}, u32[]{:S(2)}) collective-permute-start(bf16[256,512]{1,0:T(8,128)(2,1)S(1)} %collective-permute-done.2), channel_id=1, source_target_pairs={{0,1},{1,2},{2,3},{3,4},{4,5},{5,6},{6,7},{7,0},{8,9},{9,10},{10,1... | collective-permute-start | bytes 786440 | tf_op jit(solution)/shard_map/ppermute | solution.py:29
  39.0 28.8 %copy-start.10 = (f32[4096]{0:T(1024)S(1)}, f32[4096]{0:T(1024)}, u32[]{:S(2)}) copy-start(f32[4096]{0:T(1024)} %param.18) | copy-start | bytes 49156
  39.0 13.7 %collective-permute-start.6 = (bf16[256,512]{1,0:T(8,128)(2,1)S(1)}, bf16[256,512]{1,0:T(8,128)(2,1)S(1)}, u32[]{:S(2)}, u32[]{:S(2)}) collective-permute-start(bf16[256,512]{1,0:T(8,128)(2,1)S(1)} %collective-permute-done.5), channel_id=1, source_target_pairs={{0,7},{1,0},{2,1},{3,2},{4,3},{5,4},{6,5},{7,6},{8,15},{9,8},{10,9... | collective-permute-start | bytes 786440 | tf_op jit(solution)/shard_map/ppermute | solution.py:33
  59.5 12.4 %copy-start.3 = (bf16[256,128]{1,0:T(8,128)(2,1)S(1)}, bf16[256,128]{1,0:T(8,128)(2,1)}, u32[]{:S(2)}) copy-start(bf16[256,128]{1,0:T(8,128)(2,1)} %param.20) | copy-start | bytes 196612
  59.5 14.2 %copy-start.8 = (f32[256,8]{0,1:T(8,128)S(1)}, f32[256,8]{0,1:T(8,128)}, u32[]{:S(2)}) copy-start(f32[256,8]{0,1:T(8,128)} %param.21) | copy-start | bytes 24580
  73.0 93.7 %all-gather.13.cloned.1.call-start = ((), (), s32[]{:S(2)}) async-start(), calls=%async_computation.6 | async-start | bytes 2359296 | tf_op jit(solution)/shard_map/all_gather | solution.py:134
  73.7 192.5 %reduce-scatter.10.cloned.1.call-start = ((), (), s32[]{:S(2)}) async-start(), calls=%async_computation.9 | async-start | bytes 4325376
  178.0 0.9 copy-start.7
  178.0 89.3 %copy-start.9 = (f32[512]{0:T(512)S(1)}, f32[512]{0:T(512)}, u32[]{:S(2)}) copy-start(f32[512]{0:T(512)} %param.16) | copy-start | bytes 6148
  178.0 145.0 %copy-start.1 = (bf16[256,4096]{1,0:T(8,128)(2,1)S(1)}, bf16[256,4096]{1,0:T(8,128)(2,1)}, u32[]{:S(2)}) copy-start(bf16[256,4096]{1,0:T(8,128)(2,1)} %all-gather.13.cloned.1.call-done) | copy-start | bytes 6291460
  178.1 145.0 %all-gather.11.cloned.1.call-start = ((), (), s32[]{:S(2)}) async-start(), calls=%async_computation.4 | async-start | bytes 4325376 | tf_op jit(solution)/shard_map/all_gather | solution.py:132
  268.2 60.3 %copy-start.6 = (f32[256,256]{1,0:T(8,128)S(1)}, f32[256,256]{1,0:T(8,128)}, u32[]{:S(2)}) copy-start(f32[256,256]{1,0:T(8,128)} %copy-done.5) | copy-start | bytes 786436
  268.2 111.2 %all-gather.17.cloned.1.call-start = ((), (), s32[]{:S(2)}) async-start(), calls=%async_computation.8 | async-start | bytes 4325376 | tf_op jit(solution)/shard_map/all_gather | solution.py:50
  328.4 185.6 %reduce-scatter.12.cloned.1.call-start = ((), (), s32[]{:S(2)}) async-start(), calls=%async_computation.10 | async-start | bytes 4325376
  393.2 165.9 %reduce-scatter.8.cloned.1.call-start = ((), (), s32[]{:S(2)}) async-start(), calls=%async_computation.5 | async-start | bytes 2359296 | tf_op jit(solution)/shard_map/reduce_scatter | solution.py:195
  (2 other events, 1.5 us)
Sparse Core Ops, SparseCore 0:
  11.1 56.6 all-gather.8
  73.1 50.8 all-gather.14
  125.8 40.8 all-gather.12
  178.2 88.0 reduce-scatter.9
  269.5 53.5 all-gather.10
  328.6 50.7 all-gather.16
  393.3 120.6 reduce-scatter.11
  517.2 41.8 reduce-scatter.7
